TPU v7x, 512 devices: a whole 4x8x8 slice. The times are simulated.
512 devices in a mesh: head: 8 (over x, core), blk: 64 (over y, z).
Axes of the slice: x: 4, y: 8, z: 8, core: 2. Of those that a mesh axis runs over, the one named last changes fastest.
Arguments:
- suffix_hidden: bfloat16 [1536, 2048], P('blk'), may hold values from -400 to 400
- prefix_hidden: bfloat16 [16384, 2048], P('blk'), may hold values from -400 to 400
- kv_cache: bfloat16 [2, 16384, 8, 256], P(None, 'blk', 'head'), may hold values from -300 to 300
- norm_gain: float32 [2048], replicated, may hold values from 0.1 to 1.9
- norm_bias: float32 [2048], replicated, may hold values from -3 to 3
- qkv_weight: bfloat16 [2048, 8, 768], P('blk', 'head'), may hold values from -0.125 to 0.125
- qkv_bias: float32 [8, 768], P('head'), may hold values from -3 to 3
- out_weight: bfloat16 [8, 256, 2048], P('head', 'blk'), may hold values from -0.125 to 0.125
- out_bias: float32 [2048], replicated, may hold values from -3 to 3
- suffix_lengths: int32 [4], replicated, may hold values from 1 to 768, 1536 in all
- prefix_blocks: int32 [4], replicated, may hold values from 1 to 32, 64 in all
- block_owner: int32 [64], replicated, may hold values from 0 to 63, each once
- recompute_flag: int32 [16384], P('blk'), may hold values from 0 to 1, as said below
Outputs:
- attn_out: bfloat16 [1536, 2048], P('blk', 'head')
Inputs may be any that keep to these rules, and one draw needn't show every extreme that they name: `recompute_flag`: each storage block of 256 cache rows holds exactly 25 ones.
All inputs are finite; a program needn't handle non-finite values.
Results may differ from a plain program's by a relative error of at most 0.015.
Values may be sent and summed in bfloat16 or wider, within the bound.
A program may use at most 64 MiB of HBM per device.

v0:
```python
import math

import jax
import jax.numpy as jnp
from jax import lax
from jax.sharding import PartitionSpec as P

FLAG_DEV = 25


EPSILON = 1e-05
MASKED = -1e30


def layer_norm(states, norm_scale, norm_shift):
    widened = states.astype(jnp.float32)
    average = jnp.mean(widened, axis=-1, keepdims=True)
    center = widened - average
    variance = jnp.mean(center * center, axis=-1, keepdims=True)
    return (center * lax.rsqrt(variance + EPSILON) * norm_scale + norm_shift).astype(jnp.bfloat16)


def body(
    suffix_hidden,
    prefix_hidden,
    kv_cache,
    norm_gain,
    norm_bias,
    qkv_weight,
    qkv_bias,
    out_weight,
    out_bias,
    suffix_lengths,
    prefix_blocks,
    block_owner,
    recompute_flag,
):
    blk_total = lax.axis_size("blk")
    own_index = lax.axis_index("blk")
    row_count = suffix_hidden.shape[0]
    cache_rows = prefix_hidden.shape[0]
    heads_dev = qkv_weight.shape[1]
    head_dim = qkv_weight.shape[2] // 3
    total_rows = row_count * blk_total
    own_first = own_index * row_count
    tenant_ends = jnp.cumsum(suffix_lengths)
    row_ids = jnp.arange(total_rows, dtype=jnp.int32)
    row_tenant = jnp.sum((row_ids[:, None] >= tenant_ends[None, :]).astype(jnp.int32), axis=1)
    block_ends = jnp.cumsum(prefix_blocks)
    block_slots = jnp.arange(blk_total, dtype=jnp.int32)
    global_block = jnp.sum(jnp.where(block_owner == own_index, block_slots, 0))
    block_tenant = jnp.sum((global_block >= block_ends).astype(jnp.int32))
    normed = layer_norm(suffix_hidden, norm_gain, norm_bias)
    flagged = jnp.argsort(1 - recompute_flag, stable=True)[:FLAG_DEV]
    prefix_normed = layer_norm(prefix_hidden[flagged], norm_gain, norm_bias)
    fetched = lax.all_gather(qkv_weight, "blk", axis=0, tiled=True)
    piece_rows = fetched.shape[0]
    flattened = fetched.reshape(piece_rows, heads_dev * 3 * head_dim)
    kv_part = fetched[:, :, head_dim:].reshape(piece_rows, heads_dev * 2 * head_dim)
    suffix_acc = jnp.dot(normed, flattened, preferred_element_type=jnp.float32)
    prefix_acc = jnp.dot(prefix_normed, kv_part, preferred_element_type=jnp.float32)
    suffix_acc, prefix_acc = (suffix_acc, prefix_acc)
    projected = (
        (suffix_acc + qkv_bias.reshape(-1))
        .astype(jnp.bfloat16)
        .reshape(row_count, heads_dev, 3 * head_dim)
    )
    recomputed = (
        (prefix_acc + qkv_bias[:, head_dim:].reshape(-1))
        .astype(jnp.bfloat16)
        .reshape(FLAG_DEV, heads_dev, 2 * head_dim)
    )
    own_queries = projected[:, :, :head_dim].reshape(row_count, heads_dev * head_dim)
    gathered = lax.all_gather(own_queries, "blk", axis=0, tiled=True)
    prefix_keys = kv_cache[0].at[flagged].set(recomputed[:, :, :head_dim])
    prefix_values = kv_cache[1].at[flagged].set(recomputed[:, :, head_dim:])
    keys_all = jnp.concatenate([prefix_keys, projected[:, :, head_dim : 2 * head_dim]], axis=0)
    values_all = jnp.concatenate([prefix_values, projected[:, :, 2 * head_dim :]], axis=0)
    own_tenant = lax.dynamic_slice_in_dim(row_tenant, own_first, row_count, 0)
    key_tenant = jnp.concatenate([jnp.full((cache_rows,), block_tenant, jnp.int32), own_tenant])
    key_position = jnp.concatenate(
        [jnp.full((cache_rows,), -1, jnp.int32), own_first + jnp.arange(row_count, dtype=jnp.int32)]
    )
    scale = head_dim ** (-0.5)
    qblock = math.gcd(total_rows, 512)
    block_total = total_rows // qblock

    def partial_block(offset):
        query_block = lax.dynamic_slice_in_dim(gathered, offset, qblock, 0).reshape(
            qblock, heads_dev, head_dim
        )
        query_tenant = lax.dynamic_slice_in_dim(row_tenant, offset, qblock, 0)
        query_position = offset + jnp.arange(qblock, dtype=jnp.int32)
        allowed = (query_tenant[:, None] == key_tenant[None, :]) & (
            key_position[None, :] <= query_position[:, None]
        )
        scores = (
            jnp.einsum("qhd,khd->hqk", query_block, keys_all, preferred_element_type=jnp.float32)
            * scale
        )
        gate = allowed[None, :, :]
        row_peak = jnp.max(jnp.where(gate, scores, MASKED), axis=2)
        weights = jnp.where(gate, jnp.exp(scores - row_peak[:, :, None]), 0.0)
        denominator = jnp.sum(weights, axis=2)
        numerator = jnp.einsum(
            "hqk,khd->qhd",
            weights.astype(jnp.bfloat16),
            values_all,
            preferred_element_type=jnp.float32,
        )
        return (numerator.reshape(qblock, heads_dev * head_dim), denominator.T, row_peak.T)

    def fill_block(step_index, buffers):
        numer_buf, denom_buf, peak_buf = buffers
        offset = step_index * qblock
        numerator, denominator, row_peak = partial_block(offset)
        numer_buf = lax.dynamic_update_slice_in_dim(numer_buf, numerator, offset, 0)
        denom_buf = lax.dynamic_update_slice_in_dim(denom_buf, denominator, offset, 0)
        peak_buf = lax.dynamic_update_slice_in_dim(peak_buf, row_peak, offset, 0)
        return (numer_buf, denom_buf, peak_buf)

    initial = (
        jnp.zeros((total_rows, heads_dev * head_dim), jnp.float32),
        jnp.zeros((total_rows, heads_dev), jnp.float32),
        jnp.full((total_rows, heads_dev), MASKED, jnp.float32),
    )
    numer_buf, denom_buf, peak_buf = lax.fori_loop(0, block_total, fill_block, initial)
    numer_view = numer_buf.reshape(blk_total, row_count, heads_dev * head_dim)
    denom_view = denom_buf.reshape(blk_total, row_count, heads_dev)
    peak_view = peak_buf.reshape(blk_total, row_count, heads_dev)
    recv_numer, recv_denom, recv_peak = (
        lax.all_to_all(numer_view, "blk", split_axis=0, concat_axis=0, tiled=True),
        lax.all_to_all(denom_view, "blk", split_axis=0, concat_axis=0, tiled=True),
        lax.all_to_all(peak_view, "blk", split_axis=0, concat_axis=0, tiled=True),
    )
    best = jnp.max(recv_peak, axis=0)
    factor = jnp.exp(recv_peak - best[None])
    summed_denom = jnp.sum(factor * recv_denom, axis=0)
    summed_numer = jnp.sum(
        recv_numer.reshape(blk_total, row_count, heads_dev, head_dim) * factor[:, :, :, None],
        axis=0,
    )
    attended = (summed_numer / summed_denom[:, :, None]).astype(jnp.bfloat16)
    fetched = lax.all_gather(out_weight, "blk", axis=1, tiled=True)
    mixed = jnp.einsum("rhd,hde->re", attended, fetched, preferred_element_type=jnp.float32)
    summed = lax.psum_scatter(
        mixed.astype(jnp.bfloat16), "head", scatter_dimension=1, tiled=True
    ).astype(jnp.float32)
    columns = summed.shape[1]
    bias_part = lax.dynamic_slice_in_dim(out_bias, lax.axis_index("head") * columns, columns, 0)
    return (summed + bias_part).astype(jnp.bfloat16)


def solution(mesh):
    return jax.shard_map(
        body,
        mesh=mesh,
        in_specs=(
            P("blk", None),
            P("blk", None),
            P(None, "blk", "head", None),
            P(),
            P(),
            P("blk", "head", None),
            P("head", None),
            P("head", "blk", None),
            P(),
            P(),
            P(),
            P(),
            P("blk"),
        ),
        out_specs=P("blk", "head"),
        check_vma=False,
    )
```

profile of v0, /device:TPU:1, one launch (start us, length us, event | category | flops | bytes accessed | tf_op | source)
XLA Modules:
  0.0 354.7 jit_solution(12156490804968114255)
XLA Ops:
  10.3 3.2 sort.17
  14.3 1.3 fusion.58
  15.6 1.3 fusion.59
  18.2 1.0 convert_reduce_fusion.1
  19.3 1.1 fusion.39
  20.7 1.0 slice_bitcast_fusion.8
  21.7 76.2 %all-gather.4.cloned.1.call-done = bf16[2048,1,768]{2,0,1:T(8,128)(2,1)} async-done(((bf16[32,1,768]{2,0,1:T(8,128)(2,1)}), bf16[2048,1,768]{2,0,1:T(8,128)(2,1)}) %all-gather.4.cloned.1.call-update) | async-done | bytes 3145744 | tf_op jit(solution)/shard_map/all_gather | solution.py:56
  97.8 2.1 fusion.28
  101.6 2.5 fusion.25
  104.0 36.4 %all-gather = bf16[1536,1,256]{2,0,1:T(8,128)(2,1)S(1)} all-gather(bf16[24,1,256]{2,0,1:T(8,128)(2,1)S(1)} %get-tuple-element.211), channel_id=2, replica_groups=mesh['head'=8,'blk'=64] {'blk'}, dimensions={0}, use_global_device_ids=true | all-gather | bytes 798720 | tf_op jit(solution)/shard_map/all_gather | solution.py:74
  142.4 11.8 %while.17 = (s32[]{:T(128)}, f32[1536,256]{1,0:T(8,128)S(1)}, f32[1536,1]{0,1:T(1,128)}, f32[1536,1]{0,1:T(1,128)}, s32[1536]{0:T(1024)}, /*index=5*/s32[280]{0:...) while((s32[]{:T(128)}, f32[1536,256]{1,0:T(8,128)S(1)}, ...), condition=%wide.region_15.16_spmd, body=%wide.region_12.15_spmd.sunk | while | flops 149380608 | bytes 2841571 | solution.py:127
  143.2 1.0 select_reduce_fusion.2
  144.2 1.4 convolution_dynamic-update-slice_fusion.2
  148.1 1.4 convolution_dynamic-update-slice_fusion.2
  152.0 1.4 convolution_dynamic-update-slice_fusion.2
  155.7 8.6 %all-to-all-start.1 = ((f32[64,24,1]{1,2,0:T(1,128)}), f32[64,24,1]{1,2,0:T(1,128)S(1)}, u32[]{:S(2)}, u32[]{:S(2)}) async-start(f32[64,24,1]{1,2,0:T(1,128)} %bitcast.20), calls=%async_computation.1 | async-start | bytes 65536 | tf_op jit(solution)/shard_map/all_to_all | solution.py:134
  165.1 10.0 %all-to-all-done.1 = f32[64,24,1]{1,2,0:T(1,128)S(1)} async-done(((f32[64,24,1]{1,2,0:T(1,128)}), f32[64,24,1]{1,2,0:T(1,128)S(1)}, u32[]{:S(2)}, u32[]{:S(2)}) %all-to-all-start.1) | async-done | bytes 6176 | tf_op jit(solution)/shard_map/all_to_all | solution.py:134
  175.2 14.6 %all_to_all.15 = f32[64,24,1]{1,2,0:T(1,128)S(1)} all-to-all(f32[64,24,1]{1,2,0:T(1,128)S(1)} %bitcast.81), channel_id=1, replica_groups=mesh['head'=8,'blk'=64] {'blk'}, dimensions={0} | all-to-all | bytes 12288 | tf_op jit(solution)/shard_map/all_to_all | solution.py:133
  189.8 4.7 %all-to-all-start = ((f32[64,24,256]{2,1,0:T(8,128)}), f32[64,24,256]{2,1,0:T(8,128)S(1)}, u32[]{:S(2)}, u32[]{:S(2)}) async-start(f32[64,24,256]{2,1,0:T(8,128)} %bitcast.74), calls=%async_computation | async-start | bytes 3145728 | tf_op jit(solution)/shard_map/all_to_all | solution.py:132
  195.4 23.2 %all-to-all-done = f32[64,24,256]{2,1,0:T(8,128)S(1)} async-done(((f32[64,24,256]{2,1,0:T(8,128)}), f32[64,24,256]{2,1,0:T(8,128)S(1)}, u32[]{:S(2)}, u32[]{:S(2)}) %all-to-all-start) | async-done | bytes 1572896 | tf_op jit(solution)/shard_map/all_to_all | solution.py:132
  218.9 90.0 %all-gather.6.cloned.1.call-done = bf16[1,256,2048]{2,0,1:T(2,128)(2,1)} async-done(((bf16[1,4,2048]{2,0,1:T(2,128)(2,1)}), bf16[1,256,2048]{2,0,1:T(2,128)(2,1)}) %all-gather.6.cloned.1.call-update) | async-done | bytes 1048592 | tf_op jit(solution)/shard_map/all_gather | solution.py:144
  308.9 2.9 convolution_convert_fusion
  312.6 34.2 %reduce-scatter.2.cloned.1.call-done = bf16[24,256]{1,0:T(8,128)(2,1)} async-done(((bf16[24,2048]{1,0:T(8,128)(2,1)}), bf16[24,256]{1,0:T(8,128)(2,1)}) %reduce-scatter.2.cloned.1.call-update) | async-done | bytes 12304 | tf_op jit(solution)/shard_map/reduce_scatter | solution.py:146
  346.8 1.3 add_convert_fusion
  (77 shorter events, 20.7 us)
Async XLA Ops:
  6.5 7.0 %copy-start = (bf16[256,2048]{1,0:T(8,128)(2,1)S(1)}, bf16[256,2048]{1,0:T(8,128)(2,1)}, u32[]{:S(2)}) copy-start(bf16[256,2048]{1,0:T(8,128)(2,1)} %param.16) | copy-start | bytes 3145732
  6.5 91.3 %slice-start = ((f32[1,768]{1,0:T(1,128)}), f32[1,512]{1,0:T(1,128)S(1)}, s32[]{:S(2)}) async-start(f32[1,768]{1,0:T(1,128)} %param.21), calls=%async_computation.7 | async-start | bytes 4096 | tf_op jit(solution)/shard_map/slice | solution.py:69
  6.5 91.3 %copy-start.7 = (f32[2048]{0:T(1024)S(1)}, f32[2048]{0:T(1024)}, u32[]{:S(2)}) copy-start(f32[2048]{0:T(1024)} %param.18) | copy-start | bytes 24580
  6.5 91.3 %copy-start.6 = (f32[2048]{0:T(1024)S(1)}, f32[2048]{0:T(1024)}, u32[]{:S(2)}) copy-start(f32[2048]{0:T(1024)} %param.19) | copy-start | bytes 24580
  6.5 91.3 %all-gather.4.cloned.1.call-start = ((), (), s32[]{:S(2)}) async-start(), calls=%async_computation.4 | async-start | bytes 3194880 | tf_op jit(solution)/shard_map/all_gather | solution.py:56
  14.1 87.4 %copy-start.2 = (bf16[24,2048]{1,0:T(8,128)(2,1)S(1)}, bf16[24,2048]{1,0:T(8,128)(2,1)}, u32[]{:S(2)}) copy-start(bf16[24,2048]{1,0:T(8,128)(2,1)} %param.15) | copy-start | bytes 294916
  14.3 6.4 %copy-start.4 = (s32[1536]{0:T(1024)}, s32[1536]{0:T(1024)S(1)}, u32[]{:S(2)}) copy-start(s32[1536]{0:T(1024)S(1)} %convert_reduce_fusion.2) | copy-start | bytes 18436
  142.4 3.1 copy-start.3
  146.4 3.1 copy-start.3
  150.3 3.1 copy-start.3
  154.2 35.5 %copy-start.1 = (f32[1536,256]{1,0:T(8,128)}, f32[1536,256]{1,0:T(8,128)S(1)}, u32[]{:S(2)}) copy-start(f32[1536,256]{1,0:T(8,128)S(1)} %get-tuple-element.178) | copy-start | bytes 4718596
  154.2 40.3 %copy-start.5 = (bf16[1,4,2048]{2,1,0:T(4,128)(2,1)S(1)}, bf16[1,4,2048]{2,1,0:T(4,128)(2,1)}, u32[]{:S(2)}) copy-start(bf16[1,4,2048]{2,1,0:T(4,128)(2,1)} %param.22) | copy-start | bytes 49156
  155.7 19.4 %all-to-all-start.1 = ((f32[64,24,1]{1,2,0:T(1,128)}), f32[64,24,1]{1,2,0:T(1,128)S(1)}, u32[]{:S(2)}, u32[]{:S(2)}) async-start(f32[64,24,1]{1,2,0:T(1,128)} %bitcast.20), calls=%async_computation.1 | async-start | bytes 65536 | tf_op jit(solution)/shard_map/all_to_all | solution.py:134
  189.8 28.9 %all-to-all-start = ((f32[64,24,256]{2,1,0:T(8,128)}), f32[64,24,256]{2,1,0:T(8,128)S(1)}, u32[]{:S(2)}, u32[]{:S(2)}) async-start(f32[64,24,256]{2,1,0:T(8,128)} %bitcast.74), calls=%async_computation | async-start | bytes 3145728 | tf_op jit(solution)/shard_map/all_to_all | solution.py:132
  194.4 114.5 %all-gather.6.cloned.1.call-start = ((), (), s32[]{:S(2)}) async-start(), calls=%async_computation.5 | async-start | bytes 2129920 | tf_op jit(solution)/shard_map/all_gather | solution.py:144
  195.2 151.6 %reduce-scatter.2.cloned.1.call-start = ((), (), s32[]{:S(2)}) async-start(), calls=%async_computation.6 | async-start | bytes 110592 | tf_op jit(solution)/shard_map/reduce_scatter | solution.py:146
Sparse Core Ops, SparseCore 0:
  10.4 87.3 all-gather.3
  198.3 110.5 all-gather.5
  312.0 34.8 reduce-scatter.1
where the time goes:
time: 356 us; the launch traced here: 355 us
  waiting for transfers between devices  234 us (66%)
  blocking collectives  51 us (14%)
  other arithmetic  15.8 us (4%)
  matrix products  14.5 us (4%)
  starting transfers between devices  13.4 us (4%)
  between operations  13.3 us (4%)
  local copies, waits for them, and re-layouts  12.2 us (3%)
    all_gather x1, waiting for transfers between devices, body(): fetched = lax.all_gather(out_weight, 'blk', axis=1, tiled=True)  90 us
    all_gather x1, waiting for transfers between devices, body(): fetched = lax.all_gather(qkv_weight, 'blk', axis=0, tiled=True)  76.2 us
    all_gather x1, blocking collectives, body(): gathered = lax.all_gather(own_queries, 'blk', axis=0, tiled=True)  36.4 us
    reduce_scatter x1, waiting for transfers between devices, body(): lax.psum_scatter(mixed.astype(jnp.bfloat16), 'head', scatter_dimension=1,...  34.2 us
    all_to_all x1, waiting for transfers between devices, body(): lax.all_to_all(numer_view, 'blk', split_axis=0, concat_axis=0, tiled=True)  23.2 us
    all_to_all x1, blocking collectives, body(): lax.all_to_all(denom_view, 'blk', split_axis=0, concat_axis=0, tiled=True)  14.6 us
    all_to_all x1, waiting for transfers between devices, body(): lax.all_to_all(peak_view, 'blk', split_axis=0, concat_axis=0, tiled=True)  10 us
    all_to_all x1, starting transfers between devices, body(): lax.all_to_all(peak_view, 'blk', split_axis=0, concat_axis=0, tiled=True)  8.62 us
  transfers between devices with their start and end apart: 5, of which 5 were waited for; matrix products, arithmetic and copies ran while one was open for 5% of the time, Pallas kernels for 0%

commit v1 on v0

--- a/solution.py
+++ b/solution.py
@@ -53,7 +53,19 @@
     normed = layer_norm(suffix_hidden, norm_gain, norm_bias)
     flagged = jnp.argsort(1 - recompute_flag, stable=True)[:FLAG_DEV]
     prefix_normed = layer_norm(prefix_hidden[flagged], norm_gain, norm_bias)
-    fetched = lax.all_gather(qkv_weight, "blk", axis=0, tiled=True)
+    qkv_rows = qkv_weight.shape[0]
+    out_rows = out_weight.shape[1]
+    model_dim = out_weight.shape[2]
+    packed_weights = jnp.concatenate(
+        [qkv_weight.reshape(1, -1), out_weight.reshape(1, -1)], axis=1
+    )
+    fetched_all = lax.all_gather(packed_weights, "blk", axis=0, tiled=True)
+    qkv_size = qkv_rows * heads_dev * 3 * head_dim
+    fetched = fetched_all[:, :qkv_size].reshape(blk_total * qkv_rows, heads_dev, 3 * head_dim)
+    out_fetched = fetched_all[:, qkv_size:].reshape(blk_total, heads_dev, out_rows, model_dim)
+    out_fetched = jnp.transpose(out_fetched, (1, 0, 2, 3)).reshape(
+        heads_dev, blk_total * out_rows, model_dim
+    )
     piece_rows = fetched.shape[0]
     flattened = fetched.reshape(piece_rows, heads_dev * 3 * head_dim)
     kv_part = fetched[:, :, head_dim:].reshape(piece_rows, heads_dev * 2 * head_dim)
@@ -125,14 +137,15 @@
         jnp.full((total_rows, heads_dev), MASKED, jnp.float32),
     )
     numer_buf, denom_buf, peak_buf = lax.fori_loop(0, block_total, fill_block, initial)
-    numer_view = numer_buf.reshape(blk_total, row_count, heads_dev * head_dim)
-    denom_view = denom_buf.reshape(blk_total, row_count, heads_dev)
-    peak_view = peak_buf.reshape(blk_total, row_count, heads_dev)
-    recv_numer, recv_denom, recv_peak = (
-        lax.all_to_all(numer_view, "blk", split_axis=0, concat_axis=0, tiled=True),
-        lax.all_to_all(denom_view, "blk", split_axis=0, concat_axis=0, tiled=True),
-        lax.all_to_all(peak_view, "blk", split_axis=0, concat_axis=0, tiled=True),
+    width = heads_dev * head_dim + 2 * heads_dev
+    packed = jnp.concatenate([numer_buf, denom_buf, peak_buf], axis=1).reshape(
+        blk_total, row_count * width
     )
+    received = lax.all_to_all(packed, "blk", split_axis=0, concat_axis=0, tiled=True)
+    received = received.reshape(blk_total, row_count, width)
+    recv_numer = received[:, :, : heads_dev * head_dim]
+    recv_denom = received[:, :, heads_dev * head_dim : heads_dev * head_dim + heads_dev]
+    recv_peak = received[:, :, heads_dev * head_dim + heads_dev :]
     best = jnp.max(recv_peak, axis=0)
     factor = jnp.exp(recv_peak - best[None])
     summed_denom = jnp.sum(factor * recv_denom, axis=0)
@@ -141,12 +154,13 @@
         axis=0,
     )
     attended = (summed_numer / summed_denom[:, :, None]).astype(jnp.bfloat16)
-    fetched = lax.all_gather(out_weight, "blk", axis=1, tiled=True)
-    mixed = jnp.einsum("rhd,hde->re", attended, fetched, preferred_element_type=jnp.float32)
-    summed = lax.psum_scatter(
-        mixed.astype(jnp.bfloat16), "head", scatter_dimension=1, tiled=True
-    ).astype(jnp.float32)
-    columns = summed.shape[1]
+    mixed = jnp.einsum("rhd,hde->re", attended, out_fetched, preferred_element_type=jnp.float32)
+    head_total = lax.axis_size("head")
+    columns = mixed.shape[1] // head_total
+    pieces = mixed.astype(jnp.bfloat16).reshape(row_count, head_total, columns)
+    pieces = jnp.transpose(pieces, (1, 0, 2))
+    exchanged = lax.all_to_all(pieces, "head", split_axis=0, concat_axis=0, tiled=True)
+    summed = jnp.sum(exchanged.astype(jnp.float32), axis=0)
     bias_part = lax.dynamic_slice_in_dim(out_bias, lax.axis_index("head") * columns, columns, 0)
     return (summed + bias_part).astype(jnp.bfloat16)
 

time: 356 us -> 289 us (0.81)
  waiting for transfers between devices: 234 us -> 119 us
  local copies, waits for them, and re-layouts: 12.2 us -> 52.2 us
  starting transfers between devices: 13.4 us -> 28.8 us
  blocking collectives: 51 us -> 38.1 us
  other arithmetic: 15.8 us -> 23.7 us
    all_gather x2 -> x1, waiting for transfers between devices: 166 us -> 92.6 us  [body(): fetched_all = lax.all_gather(packed_weights, 'blk', axis=0, tiled=True)]
    reduce_scatter x1 -> x0, waiting for transfers between devices: 34.2 us -> none  [body(): lax.psum_scatter(mixed.astype(jnp.bfloat16), 'head', scatter_dimension=1,...]
    all_to_all x2, starting transfers between devices: 13.3 us -> 28.8 us  [the longest x1 19 us: body(): lax.all_to_all(pieces, 'head', split_axis=0, concat_axis=0, tiled=True)]
    all_to_all x1 -> x0, blocking collectives: 14.6 us -> none  [body(): lax.all_to_all(denom_view, 'blk', split_axis=0, concat_axis=0, tiled=True)]
    unnamed x15 -> x23, local copies, waits for them, and re-layouts: 0.66 us -> 14.4 us
    another operation x0 -> x2, local copies, waits for them, and re-layouts: none -> 7.49 us  [the longest x1 4.83 us: body(): flattened = fetched.reshape(piece_rows, heads_dev * 3 * head_dim)]
    reshape x2 -> x3, local copies, waits for them, and re-layouts: 0.76 us -> 8.08 us  [the longest x1 4.92 us: body(): fetched_all[:, :qkv_size]]
    all_to_all x2, waiting for transfers between devices: 33.2 us -> 26.5 us  [the longest x1 22.2 us: body(): lax.all_to_all(packed, 'blk', split_axis=0, concat_axis=0, tiled=True)]
  transfers between devices with their start and end apart: 5 -> 3, of which waited for: 5 -> 3; matrix products, arithmetic and copies ran while one was open for 5% -> 7% of each run, Pallas kernels for 0% -> 0%
where the time goes in v1:
time: 289 us; the launch traced here: 287 us
  waiting for transfers between devices  119 us (41%)
  local copies, waits for them, and re-layouts  52.2 us (18%)
  blocking collectives  38.1 us (13%)
  starting transfers between devices  28.8 us (10%)
  other arithmetic  23.7 us (8%)
  between operations  13.6 us (5%)
  matrix products  11.7 us (4%)
    all_gather x1, waiting for transfers between devices, body(): fetched_all = lax.all_gather(packed_weights, 'blk', axis=0, tiled=True)  92.6 us
    all_gather x1, blocking collectives, body(): gathered = lax.all_gather(own_queries, 'blk', axis=0, tiled=True)  38.1 us
    all_to_all x1, waiting for transfers between devices, body(): lax.all_to_all(packed, 'blk', split_axis=0, concat_axis=0, tiled=True)  22.2 us
    all_to_all x1, starting transfers between devices, body(): lax.all_to_all(pieces, 'head', split_axis=0, concat_axis=0, tiled=True)  19 us
    unnamed x23, local copies, waits for them, and re-layouts  14.4 us
    all_to_all x1, starting transfers between devices, body(): lax.all_to_all(packed, 'blk', split_axis=0, concat_axis=0, tiled=True)  9.82 us
  transfers between devices with their start and end apart: 3, of which 3 were waited for; matrix products, arithmetic and copies ran while one was open for 7% of the time, Pallas kernels for 0%

profile of v1, /device:TPU:1, one launch (start us, length us, event | category | flops | bytes accessed | tf_op | source)
XLA Modules:
  0.0 287.4 jit_solution(16090769834102768445)
XLA Ops:
  16.3 3.2 %sort.17 = (s32[256]{0:T(256)}, s32[256]{0:T(256)S(1)}) sort(s32[256]{0:T(256)S(1)} %broadcast_subtract_fusion, s32[256]{0:T(256)S(1)} %iota.25), dimensions={0}, to_apply=%region_7.8 | sort | flops 2048 | bytes 4096 | tf_op jit(solution)/shard_map/jit(argsort)/sort | solution.py:54
  22.6 92.6 %all-gather.4.cloned.1.call-done = bf16[64,1,32768]{2,1,0:T(2,128)(2,1)} async-done(((bf16[1,1,32768]{2,1,0:T(2,128)(2,1)}), bf16[64,1,32768]{2,1,0:T(2,128)(2,1)}) %all-gather.4.cloned.1.call-update) | async-done | bytes 4194320 | tf_op jit(solution)/shard_map/all_gather | solution.py:62
  115.2 7.9 %copy.55 = bf16[64,1,32768]{2,0,1:T(8,128)(2,1)S(1)} copy(bf16[64,1,32768]{2,1,0:T(2,128)(2,1)} %all-gather.4.cloned.1.call-done) | data formatting | bytes 8388608
  123.2 1.9 copy-done.1
  125.1 1.9 slice.62
  127.0 4.8 %reshape_reshape.3 = bf16[2048,768]{1,0:T(8,128)(2,1)} reshape(bf16[64,24576]{1,0:T(8,128)(2,1)} %slice.62) | data formatting | bytes 6291456 | tf_op jit(solution)/shard_map/reshape;reshape | solution.py:70
  131.8 4.9 %reshape.221 = bf16[2048,1,768]{2,0,1:T(8,128)(2,1)} reshape(bf16[64,24576]{1,0:T(8,128)(2,1)} %slice.62) | data formatting | bytes 6291456 | tf_op jit(solution)/shard_map/reshape | solution.py:64
  136.7 2.6 fusion.19
  139.4 38.1 %all-gather = bf16[1536,1,256]{2,0,1:T(8,128)(2,1)S(1)} all-gather(bf16[24,1,256]{2,0,1:T(8,128)(2,1)S(1)} %get-tuple-element.212), channel_id=2, replica_groups=mesh['head'=8,'blk'=64] {'blk'}, dimensions={0}, use_global_device_ids=true | all-gather | bytes 798720 | tf_op jit(solution)/shard_map/all_gather | solution.py:86
  181.7 11.9 %while.17 = (s32[]{:T(128)}, f32[1536,256]{1,0:T(8,128)S(1)}, f32[1536,1]{0,1:T(1,128)}, f32[1536,1]{0,1:T(1,128)}, s32[1536]{0:T(1024)}, /*index=5*/s32[280]{0:...) while((s32[]{:T(128)}, f32[1536,256]{1,0:T(8,128)S(1)}, ...), condition=%wide.region_15.16_spmd, body=%wide.region_12.15_spmd.sunk | while | flops 149380608 | bytes 2841579 | solution.py:139
  193.6 1.9 copy.40
  195.5 1.9 copy.39
  197.4 2.2 pad_maximum_fusion
  199.6 4.3 %all_to_all.12 = f32[64,1,6192]{2,1,0:T(1,128)} reshape(f32[1536,258]{1,0:T(8,128)S(1)} %pad_maximum_fusion) | data formatting | bytes 3170304 | tf_op jit(solution)/shard_map/all_to_all | solution.py:144
  203.9 9.8 %all-to-all-start = ((f32[64,1,6192]{2,1,0:T(1,128)}), f32[64,1,6192]{2,1,0:T(1,128)S(1)}, u32[]{:S(2)}, u32[]{:S(2)}) async-start(f32[64,1,6192]{2,1,0:T(1,128)} %all_to_all.12), calls=%async_computation | async-start | bytes 3211264 | tf_op jit(solution)/shard_map/all_to_all | solution.py:144
  213.7 2.3 slice.72
  216.0 2.7 reshape.225
  218.7 22.2 %all-to-all-done = f32[64,1,6192]{2,1,0:T(1,128)S(1)} async-done(((f32[64,1,6192]{2,1,0:T(1,128)}), f32[64,1,6192]{2,1,0:T(1,128)S(1)}, u32[]{:S(2)}, u32[]{:S(2)}) %all-to-all-start) | async-done | bytes 1585184 | tf_op jit(solution)/shard_map/all_to_all | solution.py:144
  240.9 5.4 %reduce.14 = f32[64,6192]{1,0:T(8,128)} reduce(f32[64,1,6192]{2,1,0:T(1,128)S(1)} %all-to-all-done, f32[]{:T(128)} %constant.108), dimensions={1}, to_apply=%all_to_all.10.reduce_sub_computation | reduce | bytes 3170308 | tf_op jit(solution)/shard_map/all_to_all | solution.py:144
  246.3 2.5 reshape.224
  248.8 1.5 fusion.51
  253.8 1.5 convolution_convert_fusion
  255.9 19.0 %all-to-all-start.1 = ((bf16[8,24,256]{2,1,0:T(8,128)(2,1)}), bf16[8,24,256]{2,1,0:T(8,128)(2,1)S(1)}, u32[]{:S(2)}, u32[]{:S(2)}) async-start(bf16[8,24,256]{2,1,0:T(8,128)(2,1)} %bitcast.70), calls=%async_computation.1 | async-start | bytes 196608 | tf_op jit(solution)/shard_map/all_to_all | solution.py:162
  275.7 4.2 %all-to-all-done.1 = bf16[8,24,256]{2,1,0:T(8,128)(2,1)S(1)} async-done(((bf16[8,24,256]{2,1,0:T(8,128)(2,1)}), bf16[8,24,256]{2,1,0:T(8,128)(2,1)S(1)}, u32[]{:S(2)}, u32[]{:S(2)}) %all-to-all-start.1) | async-done | bytes 98336 | tf_op jit(solution)/shard_map/all_to_all | solution.py:162
  (89 shorter events, 34.4 us)
Async XLA Ops:
  6.5 12.9 %copy-start = (bf16[256,2048]{1,0:T(8,128)(2,1)S(1)}, bf16[256,2048]{1,0:T(8,128)(2,1)}, u32[]{:S(2)}) copy-start(bf16[256,2048]{1,0:T(8,128)(2,1)} %param.16) | copy-start | bytes 3145732
  6.5 16.1 %copy-start.5 = (bf16[2,256,1,256]{3,1,2,0:T(8,128)(2,1)S(1)}, bf16[2,256,1,256]{3,1,2,0:T(8,128)(2,1)}, u32[]{:S(2)}) copy-start(bf16[2,256,1,256]{3,1,2,0:T(8,128)(2,1)} %param.17) | copy-start | bytes 786436
  6.5 108.7 %all-gather.4.cloned.1.call-start = ((), (), s32[]{:S(2)}) async-start(), calls=%async_computation.2 | async-start | bytes 8519680 | tf_op jit(solution)/shard_map/all_gather | solution.py:62
  11.5 1.5 copy-start.7
  123.1 1.9 copy-start.1
  131.8 4.9 %copy-start.4 = (bf16[24,2048]{1,0:T(8,128)(2,1)S(1)}, bf16[24,2048]{1,0:T(8,128)(2,1)}, u32[]{:S(2)}) copy-start(bf16[24,2048]{1,0:T(8,128)(2,1)} %param.15) | copy-start | bytes 294916
  131.8 4.9 %copy-start.8 = (f32[2048]{0:T(1024)S(1)}, f32[2048]{0:T(1024)}, u32[]{:S(2)}) copy-start(f32[2048]{0:T(1024)} %param.19) | copy-start | bytes 24580
  131.8 4.9 %copy-start.9 = (f32[2048]{0:T(1024)S(1)}, f32[2048]{0:T(1024)}, u32[]{:S(2)}) copy-start(f32[2048]{0:T(1024)} %param.18) | copy-start | bytes 24580
  136.7 40.7 %copy-start.3 = (bf16[2048,1,768]{2,0,1:T(8,128)(2,1)S(1)}, bf16[2048,1,768]{2,0,1:T(8,128)(2,1)}, u32[]{:S(2)}) copy-start(bf16[2048,1,768]{2,0,1:T(8,128)(2,1)} %reshape.221) | copy-start | bytes 9437188
  136.7 40.7 %slice-start = ((f32[1,768]{1,0:T(1,128)}), f32[1,512]{1,0:T(1,128)S(1)}, s32[]{:S(2)}) async-start(f32[1,768]{1,0:T(1,128)} %param.21), calls=%async_computation.3 | async-start | bytes 4096 | tf_op jit(solution)/shard_map/slice | solution.py:81
  181.7 3.2 %copy-start.6 = (s32[280]{0:T(512)S(1)}, s32[280]{0:T(512)}, u32[]{:S(2)}) copy-start(s32[280]{0:T(512)} %get-tuple-element.320) | copy-start | bytes 3364 | tf_op jit(solution)/shard_map/while
  185.7 3.2 %copy-start.6 = (s32[280]{0:T(512)S(1)}, s32[280]{0:T(512)}, u32[]{:S(2)}) copy-start(s32[280]{0:T(512)} %get-tuple-element.320) | copy-start | bytes 3364 | tf_op jit(solution)/shard_map/while
  189.7 3.1 %copy-start.6 = (s32[280]{0:T(512)S(1)}, s32[280]{0:T(512)}, u32[]{:S(2)}) copy-start(s32[280]{0:T(512)} %get-tuple-element.320) | copy-start | bytes 3364 | tf_op jit(solution)/shard_map/while
  193.6 3.8 %copy-start.2 = (f32[1536,256]{1,0:T(8,128)}, f32[1536,256]{1,0:T(8,128)S(1)}, u32[]{:S(2)}) copy-start(f32[1536,256]{1,0:T(8,128)S(1)} %get-tuple-element.178) | copy-start | bytes 4718596
  203.9 37.0 %all-to-all-start = ((f32[64,1,6192]{2,1,0:T(1,128)}), f32[64,1,6192]{2,1,0:T(1,128)S(1)}, u32[]{:S(2)}, u32[]{:S(2)}) async-start(f32[64,1,6192]{2,1,0:T(1,128)} %all_to_all.12), calls=%async_computation | async-start | bytes 3211264 | tf_op jit(solution)/shard_map/all_to_all | solution.py:144
  255.9 24.0 %all-to-all-start.1 = ((bf16[8,24,256]{2,1,0:T(8,128)(2,1)}), bf16[8,24,256]{2,1,0:T(8,128)(2,1)S(1)}, u32[]{:S(2)}, u32[]{:S(2)}) async-start(bf16[8,24,256]{2,1,0:T(8,128)(2,1)} %bitcast.70), calls=%async_computation.1 | async-start | bytes 196608 | tf_op jit(solution)/shard_map/all_to_all | solution.py:162
Sparse Core Ops, SparseCore 0:
  10.4 104.8 all-gather.3

commit v2 on v1

--- a/solution.py
+++ b/solution.py
@@ -6,6 +6,7 @@
 from jax.sharding import PartitionSpec as P
 
 FLAG_DEV = 25
+BLK = ("blk_hi", "blk_lo")
 
 
 EPSILON = 1e-05
@@ -18,6 +19,11 @@
     center = widened - average
     variance = jnp.mean(center * center, axis=-1, keepdims=True)
     return (center * lax.rsqrt(variance + EPSILON) * norm_scale + norm_shift).astype(jnp.bfloat16)
+
+
+def gather_blk(piece):
+    inner = lax.all_gather(piece, "blk_lo", axis=0, tiled=True)
+    return lax.all_gather(inner, "blk_hi", axis=0, tiled=True)
 
 
 def body(
@@ -35,8 +41,8 @@
     block_owner,
     recompute_flag,
 ):
-    blk_total = lax.axis_size("blk")
-    own_index = lax.axis_index("blk")
+    blk_total = lax.axis_size(BLK)
+    own_index = lax.axis_index(BLK)
     row_count = suffix_hidden.shape[0]
     cache_rows = prefix_hidden.shape[0]
     heads_dev = qkv_weight.shape[1]
@@ -56,13 +62,18 @@
     qkv_rows = qkv_weight.shape[0]
     out_rows = out_weight.shape[1]
     model_dim = out_weight.shape[2]
+    out_lanes = heads_dev * out_rows * model_dim // qkv_rows
     packed_weights = jnp.concatenate(
-        [qkv_weight.reshape(1, -1), out_weight.reshape(1, -1)], axis=1
-    )
-    fetched_all = lax.all_gather(packed_weights, "blk", axis=0, tiled=True)
-    qkv_size = qkv_rows * heads_dev * 3 * head_dim
-    fetched = fetched_all[:, :qkv_size].reshape(blk_total * qkv_rows, heads_dev, 3 * head_dim)
-    out_fetched = fetched_all[:, qkv_size:].reshape(blk_total, heads_dev, out_rows, model_dim)
+        [
+            qkv_weight.reshape(qkv_rows, heads_dev * 3 * head_dim),
+            out_weight.reshape(qkv_rows, out_lanes),
+        ],
+        axis=1,
+    )
+    fetched_all = gather_blk(packed_weights)
+    qkv_cols = heads_dev * 3 * head_dim
+    fetched = fetched_all[:, :qkv_cols].reshape(blk_total * qkv_rows, heads_dev, 3 * head_dim)
+    out_fetched = fetched_all[:, qkv_cols:].reshape(blk_total, heads_dev, out_rows, model_dim)
     out_fetched = jnp.transpose(out_fetched, (1, 0, 2, 3)).reshape(
         heads_dev, blk_total * out_rows, model_dim
     )
@@ -83,7 +94,7 @@
         .reshape(FLAG_DEV, heads_dev, 2 * head_dim)
     )
     own_queries = projected[:, :, :head_dim].reshape(row_count, heads_dev * head_dim)
-    gathered = lax.all_gather(own_queries, "blk", axis=0, tiled=True)
+    gathered = gather_blk(own_queries)
     prefix_keys = kv_cache[0].at[flagged].set(recomputed[:, :, :head_dim])
     prefix_values = kv_cache[1].at[flagged].set(recomputed[:, :, head_dim:])
     keys_all = jnp.concatenate([prefix_keys, projected[:, :, head_dim : 2 * head_dim]], axis=0)
@@ -141,7 +152,7 @@
     packed = jnp.concatenate([numer_buf, denom_buf, peak_buf], axis=1).reshape(
         blk_total, row_count * width
     )
-    received = lax.all_to_all(packed, "blk", split_axis=0, concat_axis=0, tiled=True)
+    received = lax.all_to_all(packed, BLK, split_axis=0, concat_axis=0, tiled=True)
     received = received.reshape(blk_total, row_count, width)
     recv_numer = received[:, :, : heads_dev * head_dim]
     recv_denom = received[:, :, heads_dev * head_dim : heads_dev * head_dim + heads_dev]
@@ -166,24 +177,40 @@
 
 
 def solution(mesh):
-    return jax.shard_map(
+    blk_size = mesh.shape["blk"]
+    blk_hi = math.isqrt(blk_size)
+    while blk_size % blk_hi:
+        blk_hi -= 1
+    split = jax.sharding.Mesh(
+        mesh.devices.reshape(mesh.shape["head"], blk_hi, blk_size // blk_hi),
+        ("head", "blk_hi", "blk_lo"),
+    )
+    inner = jax.shard_map(
         body,
-        mesh=mesh,
+        mesh=split,
         in_specs=(
-            P("blk", None),
-            P("blk", None),
-            P(None, "blk", "head", None),
-            P(),
-            P(),
-            P("blk", "head", None),
+            P(BLK, None),
+            P(BLK, None),
+            P(None, BLK, "head", None),
+            P(),
+            P(),
+            P(BLK, "head", None),
             P("head", None),
-            P("head", "blk", None),
-            P(),
-            P(),
-            P(),
-            P(),
-            P("blk"),
+            P("head", BLK, None),
+            P(),
+            P(),
+            P(),
+            P(),
+            P(BLK),
         ),
-        out_specs=P("blk", "head"),
+        out_specs=P(BLK, "head"),
         check_vma=False,
     )
+
+    def run(*args):
+        out = inner(*args)
+        return jax.lax.with_sharding_constraint(
+            out, jax.sharding.NamedSharding(mesh, P("blk", "head"))
+        )
+
+    return run

time: 289 us -> 255 us (0.88)
  waiting for transfers between devices: 119 us -> 76.9 us
  blocking collectives: 38.1 us -> 69.8 us
  local copies, waits for them, and re-layouts: 52.2 us -> 30 us
    all_gather x1, waiting for transfers between devices: 92.6 us -> 50 us  [gather_blk(): return lax.all_gather(inner, 'blk_hi', axis=0, tiled=True)]
    all_gather x1 -> x3, blocking collectives: 38.1 us -> 69.8 us  [the longest x2 49 us: gather_blk(): inner = lax.all_gather(piece, 'blk_lo', axis=0, tiled=True)]
    unnamed x23 -> x18, local copies, waits for them, and re-layouts: 14.4 us -> 2.9 us
    another operation x2 -> x1, local copies, waits for them, and re-layouts: 7.49 us -> 2.33 us  [run(): out = inner(*args)]
    reshape x1 -> x2, local copies, waits for them, and re-layouts: 4.92 us -> 1.17 us  [the longest x1 0.83 us: body(): out_weight.reshape(qkv_rows, out_lanes)]
where the time goes in v2:
time: 255 us; the launch traced here: 254 us
  waiting for transfers between devices  76.9 us (30%)
  blocking collectives  69.8 us (27%)
  local copies, waits for them, and re-layouts  30 us (12%)
  starting transfers between devices  27.9 us (11%)
  other arithmetic  23.8 us (9%)
  between operations  13.6 us (5%)
  matrix products  11.7 us (5%)
    all_gather x1, waiting for transfers between devices, gather_blk(): return lax.all_gather(inner, 'blk_hi', axis=0, tiled=True)  50 us
    all_gather x2, blocking collectives, gather_blk(): inner = lax.all_gather(piece, 'blk_lo', axis=0, tiled=True)  49 us
    all_to_all x1, waiting for transfers between devices, body(): lax.all_to_all(packed, BLK, split_axis=0, concat_axis=0, tiled=True)  22.7 us
    all_gather x1, blocking collectives, gather_blk(): return lax.all_gather(inner, 'blk_hi', axis=0, tiled=True)  20.8 us
    all_to_all x1, starting transfers between devices, body(): lax.all_to_all(pieces, 'head', split_axis=0, concat_axis=0, tiled=True)  18.9 us
    all_to_all x1, starting transfers between devices, body(): lax.all_to_all(packed, BLK, split_axis=0, concat_axis=0, tiled=True)  9.04 us
    all_to_all x1, other arithmetic, body(): lax.all_to_all(packed, BLK, split_axis=0, concat_axis=0, tiled=True)  5.4 us
  transfers between devices with their start and end apart: 3, of which 3 were waited for; matrix products, arithmetic and copies ran while one was open for 7% of the time, Pallas kernels for 0%

profile of v2, /device:TPU:1, one launch (start us, length us, event | category | flops | bytes accessed | tf_op | source)
XLA Modules:
  0.0 253.9 jit_solution(4083771200314557492)
XLA Ops:
  8.2 28.4 %all_gather.12 = bf16[256,1024]{1,0:T(8,128)(2,1)} all-gather(bf16[32,1024]{1,0:T(8,128)(2,1)S(1)} %pad_maximum_fusion.3), channel_id=1, replica_groups=mesh['head'=8,'blk_hi'=8,'blk_lo'=8] {'blk_lo'}, dimensions={0}, use_global_device_ids=true | all-gather | bytes 589824 | tf_op jit(solution)/shard_map/all_gather | solution.py:25
  39.7 3.2 %sort.17 = (s32[256]{0:T(256)}, s32[256]{0:T(256)S(1)}) sort(s32[256]{0:T(256)S(1)} %broadcast_subtract_fusion, s32[256]{0:T(256)S(1)} %iota.25), dimensions={0}, to_apply=%region_7.8 | sort | flops 2048 | bytes 4096 | tf_op jit(solution)/shard_map/jit(argsort)/sort | solution.py:60
  48.2 50.0 %all-gather.4.cloned.1.call-done = bf16[2048,1024]{1,0:T(8,128)(2,1)} async-done(((bf16[256,1024]{1,0:T(8,128)(2,1)}), bf16[2048,1024]{1,0:T(8,128)(2,1)}) %all-gather.4.cloned.1.call-update) | async-done | bytes 4194320 | tf_op jit(solution)/shard_map/all_gather | solution.py:26
  98.3 2.6 %fusion.26 = bf16[24,1,768]{2,0,1:T(8,128)(2,1)S(1)} fusion(bf16[2048,1024]{1,0:T(8,128)(2,1)} %all-gather.4.cloned.1.call-done, bf16[24,2048]{1,0:T(8,128)(2,1)S(1)} %copy-done.3, f32[2048]{0:T(1024)S(1)} %copy-done.6, f32[2048]{0:T(1024)S(1)} %copy-done.7, f32[24]{0:T(128)S(1)} %add_rsqrt_fusion.1, f32[24]{0:T(128)S(1)} %broadcast_multiply_fusion.1, ...), kind=kOutput, calls=%fused_computation.37 | convolution fusion | flops 75829248 | bytes 3300544 | tf_op jit(solution)/shard_map/dot_general | solution.py:83
  100.9 20.6 %all-gather = bf16[192,1,256]{2,0,1:T(8,128)(2,1)S(1)} all-gather(bf16[24,1,256]{2,0,1:T(8,128)(2,1)S(1)} %get-tuple-element.212), channel_id=2, replica_groups=mesh['head'=8,'blk_hi'=8,'blk_lo'=8] {'blk_lo'}, dimensions={0}, use_global_device_ids=true | all-gather | bytes 110592 | tf_op jit(solution)/shard_map/all_gather | solution.py:25
  121.5 20.8 %all-gather.1 = bf16[1536,1,256]{2,0,1:T(8,128)(2,1)S(1)} all-gather(bf16[192,1,256]{2,0,1:T(8,128)(2,1)S(1)} %all-gather), channel_id=3, replica_groups=mesh['head'=8,'blk_hi'=8,'blk_lo'=8] {'blk_hi'}, dimensions={0}, use_global_device_ids=true | all-gather | bytes 884736 | tf_op jit(solution)/shard_map/all_gather | solution.py:26
  147.0 13.8 %while.17 = (s32[]{:T(128)}, f32[1536,256]{1,0:T(8,128)S(1)}, f32[1536,1]{0,1:T(1,128)}, f32[1536,1]{0,1:T(1,128)}, s32[1536]{0:T(1024)}, /*index=5*/s32[280]{0:...) while((s32[]{:T(128)}, f32[1536,256]{1,0:T(8,128)S(1)}, ...), condition=%wide.region_15.16_spmd, body=%wide.region_12.15_spmd.sunk | while | flops 149380608 | bytes 2837063 | solution.py:150
  154.9 1.4 convolution_dynamic-update-slice_fusion.2
  160.9 1.9 copy.40
  162.8 1.9 copy.39
  164.7 2.2 pad_maximum_fusion
  166.9 4.3 %all_to_all.12 = f32[64,1,6192]{2,1,0:T(1,128)} reshape(f32[1536,258]{1,0:T(8,128)S(1)} %pad_maximum_fusion) | data formatting | bytes 3170304 | tf_op jit(solution)/shard_map/all_to_all | solution.py:155
  171.2 9.0 %all-to-all-start = ((f32[64,1,6192]{2,1,0:T(1,128)}), f32[64,1,6192]{2,1,0:T(1,128)S(1)}, u32[]{:S(2)}, u32[]{:S(2)}) async-start(f32[64,1,6192]{2,1,0:T(1,128)} %all_to_all.12), calls=%async_computation | async-start | bytes 3211264 | tf_op jit(solution)/shard_map/all_to_all | solution.py:155
  180.3 2.3 slice.72
  182.5 2.3 reshape.225
  184.9 22.7 %all-to-all-done = f32[64,1,6192]{2,1,0:T(1,128)S(1)} async-done(((f32[64,1,6192]{2,1,0:T(1,128)}), f32[64,1,6192]{2,1,0:T(1,128)S(1)}, u32[]{:S(2)}, u32[]{:S(2)}) %all-to-all-start) | async-done | bytes 1585184 | tf_op jit(solution)/shard_map/all_to_all | solution.py:155
  207.5 5.4 %reduce.14 = f32[64,6192]{1,0:T(8,128)} reduce(f32[64,1,6192]{2,1,0:T(1,128)S(1)} %all-to-all-done, f32[]{:T(128)} %constant.112), dimensions={1}, to_apply=%all_to_all.10.reduce_sub_computation | reduce | bytes 3170308 | tf_op jit(solution)/shard_map/all_to_all | solution.py:155
  212.9 2.5 reshape.224
  215.4 1.5 fusion.60
  217.0 1.4 copy.47
  218.4 1.4 copy.46
  220.4 1.5 convolution_convert_fusion
  222.5 18.9 %all-to-all-start.1 = ((bf16[8,24,256]{2,1,0:T(8,128)(2,1)}), bf16[8,24,256]{2,1,0:T(8,128)(2,1)S(1)}, u32[]{:S(2)}, u32[]{:S(2)}) async-start(bf16[8,24,256]{2,1,0:T(8,128)(2,1)} %bitcast.62), calls=%async_computation.1 | async-start | bytes 196608 | tf_op jit(solution)/shard_map/all_to_all | solution.py:173
  242.2 4.2 %all-to-all-done.1 = bf16[8,24,256]{2,1,0:T(8,128)(2,1)S(1)} async-done(((bf16[8,24,256]{2,1,0:T(8,128)(2,1)}), bf16[8,24,256]{2,1,0:T(8,128)(2,1)S(1)}, u32[]{:S(2)}, u32[]{:S(2)}) %all-to-all-start.1) | async-done | bytes 98336 | tf_op jit(solution)/shard_map/all_to_all | solution.py:173
  (79 shorter events, 29.7 us)
Async XLA Ops:
  6.5 40.3 %copy-start = (bf16[256,2048]{1,0:T(8,128)(2,1)S(1)}, bf16[256,2048]{1,0:T(8,128)(2,1)}, u32[]{:S(2)}) copy-start(bf16[256,2048]{1,0:T(8,128)(2,1)} %param.16) | copy-start | bytes 3145732
  6.5 41.0 %copy-start.3 = (bf16[24,2048]{1,0:T(8,128)(2,1)S(1)}, bf16[24,2048]{1,0:T(8,128)(2,1)}, u32[]{:S(2)}) copy-start(bf16[24,2048]{1,0:T(8,128)(2,1)} %param.15) | copy-start | bytes 294916
  6.5 41.7 %copy-start.4 = (bf16[2,256,1,256]{3,1,2,0:T(8,128)(2,1)S(1)}, bf16[2,256,1,256]{3,1,2,0:T(8,128)(2,1)}, u32[]{:S(2)}) copy-start(bf16[2,256,1,256]{3,1,2,0:T(8,128)(2,1)} %param.17) | copy-start | bytes 786436
  6.5 91.7 %copy-start.6 = (f32[2048]{0:T(1024)S(1)}, f32[2048]{0:T(1024)}, u32[]{:S(2)}) copy-start(f32[2048]{0:T(1024)} %param.19) | copy-start | bytes 24580
  6.5 91.7 %copy-start.7 = (f32[2048]{0:T(1024)S(1)}, f32[2048]{0:T(1024)}, u32[]{:S(2)}) copy-start(f32[2048]{0:T(1024)} %param.18) | copy-start | bytes 24580
  6.5 91.7 %all-gather.4.cloned.1.call-start = ((), (), s32[]{:S(2)}) async-start(), calls=%async_computation.2 | async-start | bytes 4718592 | tf_op jit(solution)/shard_map/all_gather | solution.py:26
  43.0 57.9 %copy-start.5 = (s32[1536]{0:T(1024)}, s32[1536]{0:T(1024)S(1)}, u32[]{:S(2)}) copy-start(s32[1536]{0:T(1024)S(1)} %convert_reduce_fusion.3) | copy-start | bytes 18436
  98.3 44.0 %copy-start.2 = (bf16[2048,1024]{1,0:T(8,128)(2,1)S(1)}, bf16[2048,1024]{1,0:T(8,128)(2,1)}, u32[]{:S(2)}) copy-start(bf16[2048,1024]{1,0:T(8,128)(2,1)} %all-gather.4.cloned.1.call-done) | copy-start | bytes 12582916
  142.3 0.7 slice-start
  160.9 3.8 %copy-start.1 = (f32[1536,256]{1,0:T(8,128)}, f32[1536,256]{1,0:T(8,128)S(1)}, u32[]{:S(2)}) copy-start(f32[1536,256]{1,0:T(8,128)S(1)} %get-tuple-element.178) | copy-start | bytes 4718596
  171.2 36.3 %all-to-all-start = ((f32[64,1,6192]{2,1,0:T(1,128)}), f32[64,1,6192]{2,1,0:T(1,128)S(1)}, u32[]{:S(2)}, u32[]{:S(2)}) async-start(f32[64,1,6192]{2,1,0:T(1,128)} %all_to_all.12), calls=%async_computation | async-start | bytes 3211264 | tf_op jit(solution)/shard_map/all_to_all | solution.py:155
  222.5 23.8 %all-to-all-start.1 = ((bf16[8,24,256]{2,1,0:T(8,128)(2,1)}), bf16[8,24,256]{2,1,0:T(8,128)(2,1)S(1)}, u32[]{:S(2)}, u32[]{:S(2)}) async-start(bf16[8,24,256]{2,1,0:T(8,128)(2,1)} %bitcast.62), calls=%async_computation.1 | async-start | bytes 196608 | tf_op jit(solution)/shard_map/all_to_all | solution.py:173
Sparse Core Ops, SparseCore 0:
  36.8 61.3 all-gather.3
